TPU v7x, 32 devices: a whole 2x2x4 slice. The times are simulated.
32 devices in a mesh: group: 2 (over y), replica: 4 (over z), seq: 4 (over x, core).
Axes of the slice: x: 2, y: 2, z: 4, core: 2. Of those that a mesh axis runs over, the one named last changes fastest.
Arguments:
- features: bfloat16 [16, 2048, 1152], P(('group', 'replica'), 'seq'), may hold values from -6 to 6
- condition: bfloat16 [16, 1152], P(('group', 'replica')), may hold values from -6 to 6
- modulator: bfloat16 [1152, 6912], P('group'), may hold values from -0.1875 to 0.1875
- modulator_bias: bfloat16 [6912], P('group'), may hold values from -3 to 3
- projector: bfloat16 [1152, 3456], P('group'), may hold values from -0.1875 to 0.1875
- projector_bias: bfloat16 [2304], P('group'), may hold values from -0.29882812 to 0.29882812
- combiner: bfloat16 [1152, 1152], P('group'), may hold values from -3 to 3
- combiner_bias: bfloat16 [1152], P('group'), may hold values from -3 to 3
- expander: bfloat16 [1152, 4608], P('group'), may hold values from -0.1875 to 0.1875
- expander_bias: bfloat16 [4608], P('group'), may hold values from -3 to 3
- reducer: bfloat16 [4608, 1152], P('group'), may hold values from -0.09375 to 0.09375
- reducer_bias: bfloat16 [1152], P('group'), may hold values from -3 to 3
- cotangent: bfloat16 [16, 2048, 1152], P(('group', 'replica'), 'seq'), may hold values from -6 to 6
Outputs:
- block_output: bfloat16 [16, 2048, 1152], P(('group', 'replica'), 'seq')
- features_grad: float32 [16, 2048, 1152], P(('group', 'replica'), 'seq')
- condition_grad: float32 [16, 1152], P(('group', 'replica'))
- modulator_grad: float32 [1152, 6912], P('group')
- modulator_bias_grad: float32 [6912], P('group')
- projector_grad: float32 [1152, 3456], P('group')
- projector_bias_grad: float32 [2304], P('group')
- combiner_grad: float32 [1152, 1152], P('group')
- combiner_bias_grad: float32 [1152], P('group')
- expander_grad: float32 [1152, 4608], P('group')
- expander_bias_grad: float32 [4608], P('group')
- reducer_grad: float32 [4608, 1152], P('group')
- reducer_bias_grad: float32 [1152], P('group')
All inputs are finite; a program needn't handle non-finite values.
Results may differ from a plain program's by a relative error of at most 0.018.
Values may be sent and summed in bfloat16 or wider, within the bound.
No kernel may reach another device: no remote copies, remote signals or barrier semaphores. Data moves between devices by JAX's collectives and lax.ppermute only.
A program may use at most 448 MiB of HBM per device.

v0:
```python
from functools import partial
import jax
import jax.numpy as jnp
from jax import lax
from jax.sharding import PartitionSpec as P

HEADS = 16
HEAD_DIM = 72
HEAD_SET = 4


def normalize(values):
    centre = jnp.mean(values, -1, keepdims=True)
    centred = values - centre
    inverse = lax.rsqrt(jnp.mean(centred * centred, -1, keepdims=True) + 1e-06)
    return (centred * inverse, inverse)


def normalize_back(grad_in, normed, inverse):
    return (
        grad_in
        - jnp.mean(grad_in, -1, keepdims=True)
        - normed * jnp.mean(grad_in * normed, -1, keepdims=True)
    ) * inverse


def matmul(operand, matrix):
    return jnp.einsum("btd,de->bte", operand, matrix, preferred_element_type=jnp.float32)


def matmul_back(operand, matrix):
    return jnp.einsum("bte,de->btd", operand, matrix, preferred_element_type=jnp.float32)


def outer_sum(operand, other):
    return jnp.einsum("btd,bte->de", operand, other, preferred_element_type=jnp.float32)


def split_heads(tensor):
    return tensor.reshape(tensor.shape[0], tensor.shape[1], HEADS, HEAD_DIM)


def to_sets(tensor):
    return tensor.reshape(tensor.shape[0], -1, HEAD_SET, tensor.shape[-1]).transpose(1, 0, 2, 3)


def from_sets(tensor):
    return tensor.transpose(1, 0, 2, 3).reshape(
        tensor.shape[1], tensor.shape[0] * tensor.shape[2] * tensor.shape[3]
    )


def attend_set(packed):
    query_block, key_block, value_block = packed
    scaling = HEAD_DIM ** (-0.5)
    scores = (
        jnp.einsum("qhd,khd->hqk", query_block, key_block, preferred_element_type=jnp.float32)
        * scaling
    )
    row_max = jnp.max(scores, -1, keepdims=True)
    exponent = jnp.exp(scores - row_max)
    row_total = jnp.sum(exponent, -1, keepdims=True)
    probabilities = (exponent / row_total).astype(jnp.bfloat16)
    context = jnp.einsum(
        "hqk,khd->qhd", probabilities, value_block, preferred_element_type=jnp.float32
    )
    log_total = (row_max + jnp.log(row_total))[..., 0]
    return (context, log_total)


def attend(packed):
    query_block, key_block, value_block = packed
    context_sets, total_sets = lax.map(
        attend_set, (to_sets(query_block), to_sets(key_block), to_sets(value_block))
    )
    return (from_sets(context_sets), total_sets.reshape(HEADS, -1))


def attend_back_set(packed):
    query_block, key_block, value_block, context_block, log_total = packed
    scaling = HEAD_DIM ** (-0.5)
    scores = (
        jnp.einsum("qhd,khd->hqk", query_block, key_block, preferred_element_type=jnp.float32)
        * scaling
    )
    probabilities = jnp.exp(scores - log_total[..., None])
    probs_grad = jnp.einsum(
        "qhd,khd->hqk", context_block, value_block, preferred_element_type=jnp.float32
    )
    row_dot = jnp.sum(probabilities * probs_grad, -1, keepdims=True)
    scores_grad = (probabilities * (probs_grad - row_dot)).astype(jnp.bfloat16)
    query_grad = (
        jnp.einsum("hqk,khd->qhd", scores_grad, key_block, preferred_element_type=jnp.float32)
        * scaling
    )
    key_part = (
        jnp.einsum("hqk,qhd->khd", scores_grad, query_block, preferred_element_type=jnp.float32)
        * scaling
    )
    value_part = jnp.einsum(
        "hqk,qhd->khd",
        probabilities.astype(jnp.bfloat16),
        context_block,
        preferred_element_type=jnp.float32,
    )
    return (query_grad, key_part, value_part)


def attend_back(packed):
    query_block, key_block, value_block, context_block, log_total = packed
    total_sets = log_total.reshape(-1, HEAD_SET, log_total.shape[-1])
    query_sets, key_sets, value_sets = lax.map(
        attend_back_set,
        (
            to_sets(query_block),
            to_sets(key_block),
            to_sets(value_block),
            to_sets(context_block),
            total_sets,
        ),
    )
    return (from_sets(query_sets), from_sets(key_sets), from_sets(value_sets))


def body(
    features,
    condition,
    modulator,
    modulator_bias,
    projector,
    projector_bias,
    combiner,
    combiner_bias,
    expander,
    expander_bias,
    reducer,
    reducer_bias,
    cotangent,
):
    shards = (
        modulator,
        modulator_bias,
        projector,
        projector_bias,
        combiner,
        combiner_bias,
        expander,
        expander_bias,
        reducer,
        reducer_bias,
    )
    gathered = (
        lax.all_gather(shards[0], "group", axis=0, tiled=True),
        lax.all_gather(shards[1], "group", axis=0, tiled=True),
        lax.all_gather(shards[2], "group", axis=0, tiled=True),
        lax.all_gather(shards[3], "group", axis=0, tiled=True),
        lax.all_gather(shards[4], "group", axis=0, tiled=True),
        lax.all_gather(shards[5], "group", axis=0, tiled=True),
        lax.all_gather(shards[6], "group", axis=0, tiled=True),
        lax.all_gather(shards[7], "group", axis=0, tiled=True),
        lax.all_gather(shards[8], "group", axis=0, tiled=True),
        lax.all_gather(shards[9], "group", axis=0, tiled=True),
    )
    (
        full_modulator,
        full_mod_bias,
        full_projector,
        full_proj_bias,
        full_combiner,
        full_comb_bias,
        full_expander,
        full_exp_bias,
        full_reducer,
        full_red_bias,
    ) = gathered
    model_width = features.shape[-1]
    cond_float = condition.astype(jnp.float32)
    silu_low = jax.nn.silu(cond_float).astype(jnp.bfloat16)
    modulation = jnp.dot(
        silu_low, full_modulator, preferred_element_type=jnp.float32
    ) + full_mod_bias.astype(jnp.float32)
    pieces = [
        modulation[:, None, position * model_width : (position + 1) * model_width]
        for position in range(6)
    ]
    shift_attn, scale_attn, gate_attn, shift_mlp, scale_mlp, gate_mlp = pieces
    residual = features.astype(jnp.float32)
    normed_one, inverse_one = normalize(residual)
    attn_in = (normed_one * (1.0 + scale_attn) + shift_attn).astype(jnp.bfloat16)
    bias_float = full_proj_bias.astype(jnp.float32)
    qkv_bias = jnp.concatenate(
        [bias_float[:model_width], jnp.zeros((model_width,), jnp.float32), bias_float[model_width:]]
    )
    qkv_low = (matmul(attn_in, full_projector) + qkv_bias).astype(jnp.bfloat16)
    queries = qkv_low[..., :model_width]
    keys_own = qkv_low[..., model_width : 2 * model_width]
    values_own = qkv_low[..., 2 * model_width :]
    keys_all, values_all = (
        lax.all_gather(keys_own, "seq", axis=1, tiled=True),
        lax.all_gather(values_own, "seq", axis=1, tiled=True),
    )
    context, log_total = lax.map(
        attend, (split_heads(queries), split_heads(keys_all), split_heads(values_all))
    )
    context_low = context.astype(jnp.bfloat16)
    attn_out = matmul(context_low, full_combiner) + full_comb_bias.astype(jnp.float32)
    hidden = residual + gate_attn * attn_out
    normed_two, inverse_two = normalize(hidden)
    mlp_in = (normed_two * (1.0 + scale_mlp) + shift_mlp).astype(jnp.bfloat16)
    expanded = matmul(mlp_in, full_expander) + full_exp_bias.astype(jnp.float32)
    activated = jax.nn.gelu(expanded, approximate=True).astype(jnp.bfloat16)
    reduced = matmul(activated, full_reducer) + full_red_bias.astype(jnp.float32)
    block_output = (hidden + gate_mlp * reduced).astype(jnp.bfloat16)
    regathered = (
        lax.all_gather(shards[0], "group", axis=0, tiled=True),
        lax.all_gather(shards[1], "group", axis=0, tiled=True),
        lax.all_gather(shards[2], "group", axis=0, tiled=True),
        lax.all_gather(shards[3], "group", axis=0, tiled=True),
        lax.all_gather(shards[4], "group", axis=0, tiled=True),
        lax.all_gather(shards[5], "group", axis=0, tiled=True),
        lax.all_gather(shards[6], "group", axis=0, tiled=True),
        lax.all_gather(shards[7], "group", axis=0, tiled=True),
        lax.all_gather(shards[8], "group", axis=0, tiled=True),
        lax.all_gather(shards[9], "group", axis=0, tiled=True),
    )
    back_modulator = regathered[0]
    back_projector = regathered[2]
    back_combiner = regathered[4]
    back_expander = regathered[6]
    back_reducer = regathered[8]
    upstream = cotangent.astype(jnp.float32)
    reduced_grad = (gate_mlp * upstream).astype(jnp.bfloat16)
    gate_mlp_grad = jnp.sum(upstream * reduced, 1)
    reducer_grad = outer_sum(activated, reduced_grad)
    reducer_bias_grad = jnp.sum(reduced_grad.astype(jnp.float32), (0, 1))
    activated_grad = matmul_back(reduced_grad, back_reducer)
    unused_value, gelu_back = jax.vjp(partial(jax.nn.gelu, approximate=True), expanded)
    expanded_grad = gelu_back(activated_grad)[0].astype(jnp.bfloat16)
    expander_grad = outer_sum(mlp_in, expanded_grad)
    expander_bias_grad = jnp.sum(expanded_grad.astype(jnp.float32), (0, 1))
    mlp_in_grad = matmul_back(expanded_grad, back_expander)
    scale_mlp_grad = jnp.sum(mlp_in_grad * normed_two, 1)
    shift_mlp_grad = jnp.sum(mlp_in_grad, 1)
    hidden_grad = upstream + normalize_back(
        mlp_in_grad * (1.0 + scale_mlp), normed_two, inverse_two
    )
    attn_out_grad = (gate_attn * hidden_grad).astype(jnp.bfloat16)
    gate_attn_grad = jnp.sum(hidden_grad * attn_out, 1)
    combiner_grad = outer_sum(context_low, attn_out_grad)
    combiner_bias_grad = jnp.sum(attn_out_grad.astype(jnp.float32), (0, 1))
    context_grad = matmul_back(attn_out_grad, back_combiner).astype(jnp.bfloat16)
    keys_back, values_back = (
        lax.all_gather(keys_own, "seq", axis=1, tiled=True),
        lax.all_gather(values_own, "seq", axis=1, tiled=True),
    )
    query_grad, key_part, value_part = lax.map(
        attend_back,
        (
            split_heads(queries),
            split_heads(keys_back),
            split_heads(values_back),
            split_heads(context_grad),
            log_total,
        ),
    )
    key_grad, value_grad = (
        lax.psum_scatter(key_part, "seq", scatter_dimension=1, tiled=True),
        lax.psum_scatter(value_part, "seq", scatter_dimension=1, tiled=True),
    )
    qkv_grad = jnp.concatenate([query_grad, key_grad, value_grad], -1).astype(jnp.bfloat16)
    projector_grad = outer_sum(attn_in, qkv_grad)
    qkv_sums = jnp.sum(qkv_grad.astype(jnp.float32), (0, 1))
    projector_bias_grad = jnp.concatenate([qkv_sums[:model_width], qkv_sums[2 * model_width :]])
    attn_in_grad = matmul_back(qkv_grad, back_projector)
    scale_attn_grad = jnp.sum(attn_in_grad * normed_one, 1)
    shift_attn_grad = jnp.sum(attn_in_grad, 1)
    features_grad = hidden_grad + normalize_back(
        attn_in_grad * (1.0 + scale_attn), normed_one, inverse_one
    )
    partial_mod = jnp.concatenate(
        [
            shift_attn_grad,
            scale_attn_grad,
            gate_attn_grad,
            shift_mlp_grad,
            scale_mlp_grad,
            gate_mlp_grad,
        ],
        -1,
    )
    modulation_grad = lax.psum(partial_mod, "seq").astype(jnp.bfloat16)
    silu_grad = jnp.einsum(
        "le,de->ld", modulation_grad, back_modulator, preferred_element_type=jnp.float32
    )
    unused_silu, silu_back = jax.vjp(jax.nn.silu, cond_float)
    condition_grad = silu_back(silu_grad)[0]
    leader = (lax.axis_index("seq") == 0).astype(jnp.float32)
    modulator_grad = (
        jnp.einsum("ld,le->de", silu_low, modulation_grad, preferred_element_type=jnp.float32)
        * leader
    )
    modulator_bias_grad = jnp.sum(modulation_grad.astype(jnp.float32), 0) * leader
    summed = (
        lax.psum_scatter(
            modulator_grad.astype(jnp.bfloat16), "group", scatter_dimension=0, tiled=True
        ).astype(jnp.float32),
        lax.psum_scatter(
            modulator_bias_grad.astype(jnp.bfloat16), "group", scatter_dimension=0, tiled=True
        ).astype(jnp.float32),
        lax.psum_scatter(
            projector_grad.astype(jnp.bfloat16), "group", scatter_dimension=0, tiled=True
        ).astype(jnp.float32),
        lax.psum_scatter(
            projector_bias_grad.astype(jnp.bfloat16), "group", scatter_dimension=0, tiled=True
        ).astype(jnp.float32),
        lax.psum_scatter(
            combiner_grad.astype(jnp.bfloat16), "group", scatter_dimension=0, tiled=True
        ).astype(jnp.float32),
        lax.psum_scatter(
            combiner_bias_grad.astype(jnp.bfloat16), "group", scatter_dimension=0, tiled=True
        ).astype(jnp.float32),
        lax.psum_scatter(
            expander_grad.astype(jnp.bfloat16), "group", scatter_dimension=0, tiled=True
        ).astype(jnp.float32),
        lax.psum_scatter(
            expander_bias_grad.astype(jnp.bfloat16), "group", scatter_dimension=0, tiled=True
        ).astype(jnp.float32),
        lax.psum_scatter(
            reducer_grad.astype(jnp.bfloat16), "group", scatter_dimension=0, tiled=True
        ).astype(jnp.float32),
        lax.psum_scatter(
            reducer_bias_grad.astype(jnp.bfloat16), "group", scatter_dimension=0, tiled=True
        ).astype(jnp.float32),
    )
    totals = (
        lax.psum(summed[0].astype(jnp.bfloat16), ("replica", "seq")).astype(jnp.float32),
        lax.psum(summed[1].astype(jnp.bfloat16), ("replica", "seq")).astype(jnp.float32),
        lax.psum(summed[2].astype(jnp.bfloat16), ("replica", "seq")).astype(jnp.float32),
        lax.psum(summed[3].astype(jnp.bfloat16), ("replica", "seq")).astype(jnp.float32),
        lax.psum(summed[4].astype(jnp.bfloat16), ("replica", "seq")).astype(jnp.float32),
        lax.psum(summed[5].astype(jnp.bfloat16), ("replica", "seq")).astype(jnp.float32),
        lax.psum(summed[6].astype(jnp.bfloat16), ("replica", "seq")).astype(jnp.float32),
        lax.psum(summed[7].astype(jnp.bfloat16), ("replica", "seq")).astype(jnp.float32),
        lax.psum(summed[8].astype(jnp.bfloat16), ("replica", "seq")).astype(jnp.float32),
        lax.psum(summed[9].astype(jnp.bfloat16), ("replica", "seq")).astype(jnp.float32),
    )
    return (
        block_output,
        features_grad,
        condition_grad,
        totals[0],
        totals[1],
        totals[2],
        totals[3],
        totals[4],
        totals[5],
        totals[6],
        totals[7],
        totals[8],
        totals[9],
    )


def solution(mesh):
    return jax.shard_map(
        body,
        mesh=mesh,
        in_specs=(
            P(("group", "replica"), "seq", None),
            P(("group", "replica"), None),
            P("group", None),
            P("group"),
            P("group", None),
            P("group"),
            P("group", None),
            P("group"),
            P("group", None),
            P("group"),
            P("group", None),
            P("group"),
            P(("group", "replica"), "seq", None),
        ),
        out_specs=(
            P(("group", "replica"), "seq", None),
            P(("group", "replica"), "seq", None),
            P(("group", "replica"), None),
            P("group", None),
            P("group"),
            P("group", None),
            P("group"),
            P("group", None),
            P("group"),
            P("group", None),
            P("group"),
            P("group", None),
            P("group"),
        ),
        check_vma=False,
    )
```

profile of v0, /device:TPU:0, one launch (start us, length us, event | category | flops | bytes accessed | tf_op | source)
XLA Modules:
  0.0 2555.5 jit_solution(12768275986361563143)
XLA Ops:
  19.9 181.6 %all-gather.11.cloned.1.call-done = bf16[1152,6912]{1,0:T(8,128)(2,1)} async-done(((bf16[576,6912]{1,0:T(8,128)(2,1)}), bf16[1152,6912]{1,0:T(8,128)(2,1)}) %all-gather.11.cloned.1.call-update) | async-done | bytes 15925264 | tf_op jit(solution)/shard_map/all_gather | solution.py:153
  209.9 92.4 %all-gather.13.cloned.1.call-done = bf16[1152,3456]{1,0:T(8,128)(2,1)} async-done(((bf16[576,3456]{1,0:T(8,128)(2,1)}), bf16[1152,3456]{1,0:T(8,128)(2,1)}) %all-gather.13.cloned.1.call-update) | async-done | bytes 7962640 | tf_op jit(solution)/shard_map/all_gather | solution.py:155
  337.2 45.4 %all-gather.17.cloned.1.call-done = bf16[2,2048,1152]{2,1,0:T(8,128)(2,1)} async-done(((bf16[2,512,1152]{2,1,0:T(8,128)(2,1)}), bf16[2,2048,1152]{2,1,0:T(8,128)(2,1)}) %all-gather.17.cloned.1.call-update) | async-done | bytes 9437200 | tf_op jit(solution)/shard_map/all_gather | solution.py:200
  382.6 12.9 copy.64
  395.4 53.4 %all-gather.15.cloned.1.call-done = bf16[2,2048,1152]{2,1,0:T(8,128)(2,1)} async-done(((bf16[2,512,1152]{2,1,0:T(8,128)(2,1)}), bf16[2,2048,1152]{2,1,0:T(8,128)(2,1)}) %all-gather.15.cloned.1.call-update) | async-done | bytes 9437200 | tf_op jit(solution)/shard_map/all_gather | solution.py:199
  448.8 12.8 copy.63
  461.6 132.3 %while.53 = (s32[]{:T(128)}, bf16[2,512,1152]{1,2,0:T(8,128)(2,1)}, f32[2,16,512]{2,1,0:T(8,128)}, bf16[2,512,16,72]{1,3,2,0:T(8,128)(2,1)S(1)}, bf16[2,2048,16,...) while((s32[]{:T(128)}, bf16[2,512,1152]{1,2,0:T(8,128)(2,1)}, ...), condition=%wide.region_7.8_spmd, body=%wide.region_2.7_spmd.sunk | while | flops 1245706240 | bytes 105679224 | solution.py:202
  471.9 52.3 %while.56 = (s32[]{:T(128)}, bf16[4,512,4,72]{1,3,2,0:T(8,128)(2,1)}, f32[4,4,512]{2,1,0:T(4,128)}, bf16[4,2048,4,72]{1,3,2,0:T(8,128)(2,1)}, bf16[4,512,4,72]{1...) while((s32[]{:T(128)}, bf16[4,512,4,72]{1,3,2,0:T(8,128)(2,1)}, ...), condition=%wide.region_6.6_spmd, body=%wide.region_3.5_spmd.sunk | while | flops 1245706240 | bytes 63080592 | solution.py:73
  538.2 51.9 %while.56 = (s32[]{:T(128)}, bf16[4,512,4,72]{1,3,2,0:T(8,128)(2,1)}, f32[4,4,512]{2,1,0:T(4,128)}, bf16[4,2048,4,72]{1,3,2,0:T(8,128)(2,1)}, bf16[4,512,4,72]{1...) while((s32[]{:T(128)}, bf16[4,512,4,72]{1,3,2,0:T(8,128)(2,1)}, ...), condition=%wide.region_6.6_spmd, body=%wide.region_3.5_spmd.sunk | while | flops 1245706240 | bytes 63080592 | solution.py:73
  606.9 15.1 all-gather.21.cloned.1.call-done
  622.1 21.5 fusion.66
  643.5 111.0 %all-gather.23.cloned.1.call-done = bf16[4608,1152]{1,0:T(8,128)(2,1)} async-done(((bf16[2304,1152]{1,0:T(8,128)(2,1)}), bf16[4608,1152]{1,0:T(8,128)(2,1)}) %all-gather.23.cloned.1.call-update) | async-done | bytes 10616848 | tf_op jit(solution)/shard_map/all_gather | solution.py:161
  754.6 27.7 %fusion.122 = (bf16[4608]{0:T(1024)(128)(2,1)}, bf16[2,512,4608]{2,1,0:T(8,128)(2,1)S(1)}) fusion(f32[2,512,4608]{2,1,0:T(8,128)} %fusion.66, f32[4608]{0:T(1024)S(1)} %copy-done.32, bf16[4608,1152]{1,0:T(8,128)(2,1)} %all-gather.23.cloned.1.call-done, bf16[2,512,1152]{2,1,0:T(8,128)(2,1)S(1)} %copy-done.14, f32[2,1152]{1,0:T(2,128)S(1)} %copy-done.26), kind=kOutput, calls=%fused_computation.185 | convolution fusion | flops 10978979840 | bytes 41324544 | tf_op jit(solution)/shard_map/bte,de->btd/dot_general | solution.py:32
  786.0 17.7 fusion.64
  803.7 26.0 %fusion.90 = (f32[2,1152]{1,0:T(2,128)}, bf16[2,512,1152]{2,1,0:T(8,128)(2,1)}, f32[2,1152]{1,0:T(2,128)}, f32[2,512]{1,0:T(2,128)S(1)}, f32[2,512]{1,0:T(2,128)S(1)}, /*index=5*/f32[2,1152]{1,0:T(2,128)}) fusion(bf16[2,512,1152]{2,1,0:T(8,128)(2,1)S(1)} %copy-done.14, f32[2,512,1152]{2,1,0:T(8,128)} %copy-done.10, f32[2,1152]{1,0:T(2,128)S(1)} %copy-done.26, ...), kind=kOutput, calls=%fused_computation.123 | convolution fusion | flops 10937688064 | bytes 43732480 | tf_op jit(solution)/shard_map/btd,de->bte/dot_general | solution.py:28
  845.2 400.5 %while.55 = (s32[]{:T(128)}, bf16[2,512,1152]{2,1,0:T(8,128)(2,1)}, f32[2,2048,1152]{2,1,0:T(8,128)}, f32[2,2048,1152]{2,1,0:T(8,128)}, bf16[2,512,16,72]{1,3,2,...) while((s32[]{:T(128)}, bf16[2,512,1152]{2,1,0:T(8,128)(2,1)}, ...), condition=%wide.region_16.17_spmd, body=%wide.region_12.16_spmd.sunk | while | flops 3070965760 | bytes 315880896 | solution.py:256
  858.2 152.7 %while.57 = (s32[]{:T(128)}, bf16[4,512,4,72]{1,3,2,0:T(8,128)(2,1)}, f32[4,2048,4,72]{1,3,2,0:T(8,128)}, f32[4,2048,4,72]{1,3,2,0:T(8,128)}, bf16[4,2048,4,72]{...) while((s32[]{:T(128)}, ...), condition=%wide.region_15.15_spmd, body=%wide.region_13.14_spmd.sunk | while | flops 3070965760 | bytes 169473184 | solution.py:112
  1032.1 13.3 constant_dynamic-update-slice_fusion.18
  1058.2 152.7 %while.57 = (s32[]{:T(128)}, bf16[4,512,4,72]{1,3,2,0:T(8,128)(2,1)}, f32[4,2048,4,72]{1,3,2,0:T(8,128)}, f32[4,2048,4,72]{1,3,2,0:T(8,128)}, bf16[4,2048,4,72]{...) while((s32[]{:T(128)}, ...), condition=%wide.region_15.15_spmd, body=%wide.region_13.14_spmd.sunk | while | flops 3070965760 | bytes 169473184 | solution.py:112
  1232.2 13.3 constant_dynamic-update-slice_fusion.18
  1253.9 25.8 %fusion.52 = bf16[4608,1152]{1,0:T(8,128)(2,1)} fusion(bf16[2,512,1152]{2,1,0:T(8,128)(2,1)S(1)} %copy-done.15, f32[2,1152]{1,0:T(2,128)S(1)} %copy-done.27, f32[2,512,4608]{2,1,0:T(8,128)} %fusion.66, f32[4608]{0:T(1024)S(1)} %copy-done.33), kind=kOutput, calls=%fused_computation.75 | convolution fusion | flops 10927669248 | bytes 31878144 | tf_op jit(solution)/shard_map/btd,bte->de/dot_general | solution.py:36
  1280.5 18.6 fusion.51
  1299.1 84.6 %reduce-scatter.10.cloned.1.call-done = f32[2,512,1152]{2,1,0:T(8,128)} async-done(((f32[2,2048,1152]{2,1,0:T(8,128)}), f32[2,512,1152]{2,1,0:T(8,128)}) %reduce-scatter.10.cloned.1.call-update) | async-done | bytes 4718608 | tf_op jit(solution)/shard_map/reduce_scatter | solution.py:268
  1387.8 136.4 %reduce-scatter.8.cloned.1.call-done = f32[2,512,1152]{2,1,0:T(8,128)} async-done(((f32[2,2048,1152]{2,1,0:T(8,128)}), f32[2,512,1152]{2,1,0:T(8,128)}) %reduce-scatter.8.cloned.1.call-update) | async-done | bytes 4718608 | tf_op jit(solution)/shard_map/reduce_scatter | solution.py:267
  1528.4 12.7 fusion.60
  1541.4 16.0 fusion.87
  1584.2 107.0 %reduce-scatter.20.cloned.1.call-done = bf16[2304,1152]{1,0:T(8,128)(2,1)} async-done(((bf16[4608,1152]{1,0:T(8,128)(2,1)}), bf16[2304,1152]{1,0:T(8,128)(2,1)}) %reduce-scatter.20.cloned.1.call-update) | async-done | bytes 5308432 | tf_op jit(solution)/shard_map/reduce_scatter | solution.py:328
  1691.2 126.1 %reduce-scatter.18.cloned.1.call-done = bf16[576,4608]{1,0:T(8,128)(2,1)} async-done(((bf16[1152,4608]{1,0:T(8,128)(2,1)}), bf16[576,4608]{1,0:T(8,128)(2,1)}) %reduce-scatter.18.cloned.1.call-update) | async-done | bytes 5308432 | tf_op jit(solution)/shard_map/reduce_scatter | solution.py:322
  1817.3 97.7 %reduce-scatter.14.cloned.1.call-done = bf16[576,3456]{1,0:T(8,128)(2,1)} async-done(((bf16[1152,3456]{1,0:T(8,128)(2,1)}), bf16[576,3456]{1,0:T(8,128)(2,1)}) %reduce-scatter.14.cloned.1.call-update) | async-done | bytes 3981328 | tf_op jit(solution)/shard_map/reduce_scatter | solution.py:310
  1915.0 182.8 %reduce-scatter.12.cloned.1.call-done = bf16[576,6912]{1,0:T(8,128)(2,1)} async-done(((bf16[1152,6912]{1,0:T(8,128)(2,1)}), bf16[576,6912]{1,0:T(8,128)(2,1)}) %reduce-scatter.12.cloned.1.call-update) | async-done | bytes 7962640 | tf_op jit(solution)/shard_map/reduce_scatter | solution.py:304
  2112.0 63.2 %all-reduce.7 = (bf16[3456]{0:T(1024)(128)(2,1)S(1)}, bf16[1152]{0:T(1024)(128)(2,1)S(1)}, bf16[576]{0:T(1024)(128)(2,1)S(1)}, bf16[2304]{0:T(1024)(128)(2,1)S(1)}, bf16[576]{0:T(1024)(128)(2,1)S(1)}) all-reduce(bf16[3456]{0:T(1024)(128)(2,1)S(1)} %dynamic-slice.3, ...), channel_id=1, replica_groups=mesh['group'=2,'replica'=4,'seq'=4] {'replica','seq'}, use_global_device_ids=true, to_apply=%region_32.33 | all-reduce | flops 8064 | bytes 32256 | tf_op jit(solution)/shard_map/psum | solution.py:337
  2188.9 329.8 %all-reduce.13.cloned.1.call-done = (bf16[576,6912]{1,0:T(8,128)(2,1)}, bf16[576,3456]{1,0:T(8,128)(2,1)}, bf16[576,1152]{1,0:T(8,128)(2,1)}, bf16[576,4608]{1,0:T(8,128)(2,1)}, bf16[2304,1152]{1,0:T(8,128)(2,1)}) async-done(((bf16[576,6912]{1,0:T(8,128)(2,1)}, bf16[576,3456]{1,0:T(8,128)(2,1)}, bf16[576,1152]{1,0:T(8,128)(2,1)}, bf16[576,4608]{1,0:T(8,128)(2,1)}, bf16[2304,1152]{1,0:T(8,128)(2,1)}), ...) | async-done | bytes 23887888 | tf_op jit(solution)/shard_map/psum | solution.py:336
  (414 shorter events, 691.7 us)
Async XLA Ops:
  7.2 194.4 %all-gather.11.cloned.1.call-start = ((), (), s32[]{:S(2)}) async-start(), calls=%async_computation.7 | async-start | bytes 23887872 | tf_op jit(solution)/shard_map/all_gather | solution.py:153
  7.9 193.6 %copy-start.18 = (bf16[2,1152]{1,0:T(2,128)(2,1)S(1)}, bf16[2,1152]{1,0:T(2,128)(2,1)}, u32[]{:S(2)}) copy-start(bf16[2,1152]{1,0:T(2,128)(2,1)} %param.22) | copy-start | bytes 13828
  8.0 294.4 %all-gather.13.cloned.1.call-start = ((), (), s32[]{:S(2)}) async-start(), calls=%async_computation.8 | async-start | bytes 11943936 | tf_op jit(solution)/shard_map/all_gather | solution.py:155
  8.7 373.9 %all-gather.17.cloned.1.call-start = ((), (), s32[]{:S(2)}) async-start(), calls=%async_computation.10 | async-start | bytes 11796480 | tf_op jit(solution)/shard_map/all_gather | solution.py:200
  19.1 283.2 %copy-start.30 = (f32[2,512]{1,0:T(2,128)}, f32[2,512]{1,0:T(2,128)S(1)}, u32[]{:S(2)}) copy-start(f32[2,512]{1,0:T(2,128)S(1)} %broadcast_multiply_fusion.5) | copy-start | bytes 12292
  19.9 282.4 %copy-start.38 = (f32[2,512]{1,0:T(2,128)}, f32[2,512]{1,0:T(2,128)S(1)}, u32[]{:S(2)}) copy-start(f32[2,512]{1,0:T(2,128)S(1)} %add_rsqrt_fusion.1) | copy-start | bytes 12292
  209.9 105.1 %copy-start.22 = (f32[2,1152]{1,0:T(2,128)}, f32[2,1152]{1,0:T(2,128)S(1)}, u32[]{:S(2)}) copy-start(f32[2,1152]{1,0:T(2,128)S(1)} %get-tuple-element.313) | copy-start | bytes 27652
  209.9 105.1 %copy-start.41 = (f32[2,1152]{1,0:T(2,128)}, f32[2,1152]{1,0:T(2,128)S(1)}, u32[]{:S(2)}) copy-start(f32[2,1152]{1,0:T(2,128)S(1)} %get-tuple-element.312) | copy-start | bytes 27652
  318.2 130.6 %all-gather.15.cloned.1.call-start = ((), (), s32[]{:S(2)}) async-start(), calls=%async_computation.9 | async-start | bytes 11796480 | tf_op jit(solution)/shard_map/all_gather | solution.py:199
  318.8 275.1 %all-gather.19.cloned.1.call-start = ((), (), s32[]{:S(2)}) async-start(), calls=%async_computation.11 | async-start | bytes 3981312 | tf_op jit(solution)/shard_map/all_gather | solution.py:157
  319.4 302.6 %all-gather.21.cloned.1.call-start = ((), (), s32[]{:S(2)}) async-start(), calls=%async_computation.12 | async-start | bytes 15925248 | tf_op jit(solution)/shard_map/all_gather | solution.py:159
  320.0 434.5 %all-gather.23.cloned.1.call-start = ((), (), s32[]{:S(2)}) async-start(), calls=%async_computation.13 | async-start | bytes 15925248 | tf_op jit(solution)/shard_map/all_gather | solution.py:161
  320.7 1063.0 %reduce-scatter.10.cloned.1.call-start = ((), (), s32[]{:S(2)}) async-start(), calls=%async_computation.15 | async-start | bytes 23592960 | tf_op jit(solution)/shard_map/reduce_scatter | solution.py:268
  461.6 132.3 %copy-start.28 = (f32[2,1152]{1,0:T(2,128)S(1)}, f32[2,1152]{1,0:T(2,128)}, u32[]{:S(2)}) copy-start(f32[2,1152]{1,0:T(2,128)} %get-tuple-element.314) | copy-start | bytes 27652
  471.9 56.0 %copy-start.3 = (bf16[2,512,16,72]{1,3,2,0:T(8,128)(2,1)S(1)}, bf16[2,512,16,72]{1,3,2,0:T(8,128)(2,1)}, u32[]{:S(2)}) copy-start(bf16[2,512,16,72]{1,3,2,0:T(8,128)(2,1)} %copy-done.2) | copy-start | bytes 7077892 | tf_op jit(solution)/shard_map/while
  604.1 225.5 %copy-start.20 = (f32[2,512]{1,0:T(2,128)}, f32[2,512]{1,0:T(2,128)S(1)}, u32[]{:S(2)}) copy-start(f32[2,512]{1,0:T(2,128)S(1)} %broadcast_multiply_fusion.4) | copy-start | bytes 12292
  606.9 222.8 %copy-start.36 = (f32[2,512]{1,0:T(2,128)}, f32[2,512]{1,0:T(2,128)S(1)}, u32[]{:S(2)}) copy-start(f32[2,512]{1,0:T(2,128)S(1)} %add_rsqrt_fusion) | copy-start | bytes 12292
  622.0 132.5 %copy-start.14 = (bf16[2,512,1152]{2,1,0:T(8,128)(2,1)S(1)}, bf16[2,512,1152]{2,1,0:T(8,128)(2,1)}, u32[]{:S(2)}) copy-start(bf16[2,512,1152]{2,1,0:T(8,128)(2,1)} %param.33) | copy-start | bytes 7077892
  622.0 132.5 %copy-start.26 = (f32[2,1152]{1,0:T(2,128)S(1)}, f32[2,1152]{1,0:T(2,128)}, u32[]{:S(2)}) copy-start(f32[2,1152]{1,0:T(2,128)} %get-tuple-element.309) | copy-start | bytes 27652
  622.0 132.5 %copy-start.32 = (f32[4608]{0:T(1024)S(1)}, f32[4608]{0:T(1024)}, u32[]{:S(2)}) copy-start(f32[4608]{0:T(1024)} %reshape.180) | copy-start | bytes 55300
  1245.8 278.4 %reduce-scatter.8.cloned.1.call-start = ((), (), s32[]{:S(2)}) async-start(), calls=%async_computation.14 | async-start | bytes 23592960 | tf_op jit(solution)/shard_map/reduce_scatter | solution.py:267
  1246.5 337.7 %reduce-scatter.16.cloned.1.call-start = ((), (), s32[]{:S(2)}) async-start(), calls=%async_computation.18 | async-start | bytes 3981312 | tf_op jit(solution)/shard_map/reduce_scatter | solution.py:316
  1253.9 437.3 %reduce-scatter.20.cloned.1.call-start = ((), (), s32[]{:S(2)}) async-start(), calls=%async_computation.20 | async-start | bytes 15925248 | tf_op jit(solution)/shard_map/reduce_scatter | solution.py:328
  1279.8 537.5 %reduce-scatter.18.cloned.1.call-start = ((), (), s32[]{:S(2)}) async-start(), calls=%async_computation.19 | async-start | bytes 15925248 | tf_op jit(solution)/shard_map/reduce_scatter | solution.py:322
  1299.1 615.9 %reduce-scatter.14.cloned.1.call-start = ((), (), s32[]{:S(2)}) async-start(), calls=%async_computation.17 | async-start | bytes 11943936 | tf_op jit(solution)/shard_map/reduce_scatter | solution.py:310
  1383.7 144.7 %copy-start.23 = (f32[2,1152]{1,0:T(2,128)S(1)}, f32[2,1152]{1,0:T(2,128)}, u32[]{:S(2)}) copy-start(f32[2,1152]{1,0:T(2,128)} %copy-done.22) | copy-start | bytes 27652
  1383.7 144.7 %copy-start.31 = (f32[2,512]{1,0:T(2,128)S(1)}, f32[2,512]{1,0:T(2,128)}, u32[]{:S(2)}) copy-start(f32[2,512]{1,0:T(2,128)} %copy-done.30) | copy-start | bytes 12292
  1383.7 144.7 %copy-start.39 = (f32[2,512]{1,0:T(2,128)S(1)}, f32[2,512]{1,0:T(2,128)}, u32[]{:S(2)}) copy-start(f32[2,512]{1,0:T(2,128)} %copy-done.38) | copy-start | bytes 12292
  1383.7 144.7 %copy-start.42 = (f32[2,1152]{1,0:T(2,128)S(1)}, f32[2,1152]{1,0:T(2,128)}, u32[]{:S(2)}) copy-start(f32[2,1152]{1,0:T(2,128)} %copy-done.41) | copy-start | bytes 27652
  1387.8 140.6 %copy-start.9 = (bf16[2,512,1152]{2,1,0:T(8,128)(2,1)S(1)}, bf16[2,512,1152]{2,1,0:T(8,128)(2,1)}, u32[]{:S(2)}) copy-start(bf16[2,512,1152]{2,1,0:T(8,128)(2,1)} %param.21) | copy-start | bytes 7077892
  1541.2 556.6 %reduce-scatter.12.cloned.1.call-start = ((), (), s32[]{:S(2)}) async-start(), calls=%async_computation.16 | async-start | bytes 23887872 | tf_op jit(solution)/shard_map/reduce_scatter | solution.py:304
  1584.2 934.5 %all-reduce.13.cloned.1.call-start = ((), (), s32[]{:S(2)}) async-start(), calls=%async_computation.21 | async-start | bytes 47775744 | tf_op jit(solution)/shard_map/psum | solution.py:336
  (69 other events, 497.2 us)
Sparse Core Ops, SparseCore 0:
  9.6 191.9 all-gather.10
  203.1 99.1 all-gather.12
  318.3 64.2 all-gather.16
  384.6 64.2 all-gather.14
  450.2 39.3 all-gather.18
  491.0 130.9 all-gather.20
  623.6 130.9 all-gather.22
  1245.9 137.8 reduce-scatter.9
  1386.3 137.8 reduce-scatter.7
  1526.9 38.0 reduce-scatter.15
  1567.8 123.3 reduce-scatter.19
  1693.9 123.3 reduce-scatter.17
  1820.2 94.7 reduce-scatter.13
  1917.7 180.0 reduce-scatter.11
  2102.9 415.7 all-reduce.12
where the time goes:
time: 2570 us; the launch traced here: 2560 us
  waiting for transfers between devices  1570 us (61%)
  matrix products  518 us (20%)
  other arithmetic  177 us (7%)
  local copies, waits for them, and re-layouts  172 us (7%)
  blocking collectives  100 us (4%)
    psum x1, waiting for transfers between devices, body(): lax.psum(summed[0].astype(jnp.bfloat16), ('replica', 'seq'))  330 us
    reduce_scatter x1, waiting for transfers between devices, body(): lax.psum_scatter(modulator_grad.astype(jnp.bfloat16), 'group', scatter_di...  183 us
    all_gather x1, waiting for transfers between devices, body(): lax.all_gather(shards[0], 'group', axis=0, tiled=True)  182 us
    reduce_scatter x1, waiting for transfers between devices, body(): lax.psum_scatter(key_part, 'seq', scatter_dimension=1, tiled=True)  136 us
    reduce_scatter x1, waiting for transfers between devices, body(): lax.psum_scatter(expander_grad.astype(jnp.bfloat16), 'group', scatter_dim...  126 us
    all_gather x1, waiting for transfers between devices, body(): lax.all_gather(shards[8], 'group', axis=0, tiled=True)  111 us
    reduce_scatter x1, waiting for transfers between devices, body(): lax.psum_scatter(reducer_grad.astype(jnp.bfloat16), 'group', scatter_dime...  107 us
    reduce_scatter x1, waiting for transfers between devices, body(): lax.psum_scatter(projector_grad.astype(jnp.bfloat16), 'group', scatter_di...  97.7 us
  transfers between devices with their start and end apart: 15, of which 13 were waited for; matrix products, arithmetic and copies ran while one was open for 13% of the time, Pallas kernels for 0%

commit v1 on v0

--- a/solution.py
+++ b/solution.py
@@ -7,6 +7,7 @@
 HEADS = 16
 HEAD_DIM = 72
 HEAD_SET = 4
+ports_point = lambda x0, named_axis: lax.all_gather(x0, axis_name=named_axis).sum(axis=0)
 
 
 def normalize(values):
@@ -333,7 +334,7 @@
         ).astype(jnp.float32),
     )
     totals = (
-        lax.psum(summed[0].astype(jnp.bfloat16), ("replica", "seq")).astype(jnp.float32),
+        ports_point(summed[0].astype(jnp.bfloat16), ("replica", "seq")).astype(jnp.float32),
         lax.psum(summed[1].astype(jnp.bfloat16), ("replica", "seq")).astype(jnp.float32),
         lax.psum(summed[2].astype(jnp.bfloat16), ("replica", "seq")).astype(jnp.float32),
         lax.psum(summed[3].astype(jnp.bfloat16), ("replica", "seq")).astype(jnp.float32),

time: 2570 us -> 3070 us (1.19)
  waiting for transfers between devices: 1570 us -> 2030 us
  other arithmetic: 177 us -> 222 us
    all_gather x0 -> x1, waiting for transfers between devices: none -> 590 us  [lax.all_gather(x0, axis_name=named_axis).sum(axis=0)]
    psum x1, waiting for transfers between devices: 330 us -> 198 us  [body(): lax.psum(summed[2].astype(jnp.bfloat16), ('replica', 'seq'))]
    reduce_sum x0 -> x1, other arithmetic: none -> 43.4 us  [lax.all_gather(x0, axis_name=named_axis).sum(axis=0)]
  transfers between devices with their start and end apart: 15 -> 16, of which waited for: 13 -> 14; matrix products, arithmetic and copies ran while one was open for 13% -> 11% of each run, Pallas kernels for 0% -> 0%
where the time goes in v1:
time: 3070 us; the launch traced here: 3060 us
  waiting for transfers between devices  2030 us (66%)
  matrix products  518 us (17%)
  other arithmetic  222 us (7%)
  local copies, waits for them, and re-layouts  172 us (6%)
  blocking collectives  100 us (3%)
    all_gather x1, waiting for transfers between devices, lax.all_gather(x0, axis_name=named_axis).sum(axis=0)  590 us
    psum x1, waiting for transfers between devices, body(): lax.psum(summed[2].astype(jnp.bfloat16), ('replica', 'seq'))  198 us
    reduce_scatter x1, waiting for transfers between devices, body(): lax.psum_scatter(modulator_grad.astype(jnp.bfloat16), 'group', scatter_di...  183 us
    all_gather x1, waiting for transfers between devices, body(): lax.all_gather(shards[0], 'group', axis=0, tiled=True)  182 us
    reduce_scatter x1, waiting for transfers between devices, body(): lax.psum_scatter(key_part, 'seq', scatter_dimension=1, tiled=True)  136 us
    reduce_scatter x1, waiting for transfers between devices, body(): lax.psum_scatter(expander_grad.astype(jnp.bfloat16), 'group', scatter_dim...  126 us
    all_gather x1, waiting for transfers between devices, body(): lax.all_gather(shards[8], 'group', axis=0, tiled=True)  111 us
    reduce_scatter x1, waiting for transfers between devices, body(): lax.psum_scatter(reducer_grad.astype(jnp.bfloat16), 'group', scatter_dime...  107 us
  transfers between devices with their start and end apart: 16, of which 14 were waited for; matrix products, arithmetic and copies ran while one was open for 11% of the time, Pallas kernels for 0%

profile of v1, /device:TPU:0, one launch (start us, length us, event | category | flops | bytes accessed | tf_op | source)
XLA Modules:
  0.0 3059.1 jit_solution(12396778991393922014)
XLA Ops:
  19.9 181.6 %all-gather.13.cloned.1.call-done = bf16[1152,6912]{1,0:T(8,128)(2,1)} async-done(((bf16[576,6912]{1,0:T(8,128)(2,1)}), bf16[1152,6912]{1,0:T(8,128)(2,1)}) %all-gather.13.cloned.1.call-update) | async-done | bytes 15925264 | tf_op jit(solution)/shard_map/all_gather | solution.py:154
  209.9 92.4 %all-gather.15.cloned.1.call-done = bf16[1152,3456]{1,0:T(8,128)(2,1)} async-done(((bf16[576,3456]{1,0:T(8,128)(2,1)}), bf16[1152,3456]{1,0:T(8,128)(2,1)}) %all-gather.15.cloned.1.call-update) | async-done | bytes 7962640 | tf_op jit(solution)/shard_map/all_gather | solution.py:156
  337.1 45.4 %all-gather.19.cloned.1.call-done = bf16[2,2048,1152]{2,1,0:T(8,128)(2,1)} async-done(((bf16[2,512,1152]{2,1,0:T(8,128)(2,1)}), bf16[2,2048,1152]{2,1,0:T(8,128)(2,1)}) %all-gather.19.cloned.1.call-update) | async-done | bytes 9437200 | tf_op jit(solution)/shard_map/all_gather | solution.py:201
  382.6 12.9 copy.64
  395.4 53.4 %all-gather.17.cloned.1.call-done = bf16[2,2048,1152]{2,1,0:T(8,128)(2,1)} async-done(((bf16[2,512,1152]{2,1,0:T(8,128)(2,1)}), bf16[2,2048,1152]{2,1,0:T(8,128)(2,1)}) %all-gather.17.cloned.1.call-update) | async-done | bytes 9437200 | tf_op jit(solution)/shard_map/all_gather | solution.py:200
  461.6 132.3 %while.53 = (s32[]{:T(128)}, bf16[2,512,1152]{1,2,0:T(8,128)(2,1)}, f32[2,16,512]{2,1,0:T(8,128)}, bf16[2,512,16,72]{1,3,2,0:T(8,128)(2,1)S(1)}, bf16[2,2048,16,...) while((s32[]{:T(128)}, bf16[2,512,1152]{1,2,0:T(8,128)(2,1)}, ...), condition=%wide.region_7.8_spmd, body=%wide.region_2.7_spmd.sunk | while | flops 1245706240 | bytes 105679224 | solution.py:203
  471.9 52.3 %while.56 = (s32[]{:T(128)}, bf16[4,512,4,72]{1,3,2,0:T(8,128)(2,1)}, f32[4,4,512]{2,1,0:T(4,128)}, bf16[4,2048,4,72]{1,3,2,0:T(8,128)(2,1)}, bf16[4,512,4,72]{1...) while((s32[]{:T(128)}, bf16[4,512,4,72]{1,3,2,0:T(8,128)(2,1)}, ...), condition=%wide.region_6.6_spmd, body=%wide.region_3.5_spmd.sunk | while | flops 1245706240 | bytes 63080592 | solution.py:74
  538.2 51.9 %while.56 = (s32[]{:T(128)}, bf16[4,512,4,72]{1,3,2,0:T(8,128)(2,1)}, f32[4,4,512]{2,1,0:T(4,128)}, bf16[4,2048,4,72]{1,3,2,0:T(8,128)(2,1)}, bf16[4,512,4,72]{1...) while((s32[]{:T(128)}, bf16[4,512,4,72]{1,3,2,0:T(8,128)(2,1)}, ...), condition=%wide.region_6.6_spmd, body=%wide.region_3.5_spmd.sunk | while | flops 1245706240 | bytes 63080592 | solution.py:74
  606.9 15.1 all-gather.23.cloned.1.call-done
  622.1 21.5 fusion.66
  643.5 111.0 %all-gather.25.cloned.1.call-done = bf16[4608,1152]{1,0:T(8,128)(2,1)} async-done(((bf16[2304,1152]{1,0:T(8,128)(2,1)}), bf16[4608,1152]{1,0:T(8,128)(2,1)}) %all-gather.25.cloned.1.call-update) | async-done | bytes 10616848 | tf_op jit(solution)/shard_map/all_gather | solution.py:162
  754.6 27.7 fusion.122
  786.0 17.7 fusion.64
  803.6 26.0 fusion.90
  845.1 401.0 %while.55 = (s32[]{:T(128)}, bf16[2,512,1152]{2,1,0:T(8,128)(2,1)}, f32[2,2048,1152]{2,1,0:T(8,128)}, f32[2,2048,1152]{2,1,0:T(8,128)}, bf16[2,512,16,72]{1,3,2,...) while((s32[]{:T(128)}, bf16[2,512,1152]{2,1,0:T(8,128)(2,1)}, ...), condition=%wide.region_16.17_spmd, body=%wide.region_12.16_spmd.sunk | while | flops 3070965760 | bytes 315880896 | solution.py:257
  858.1 153.1 %while.57 = (s32[]{:T(128)}, bf16[4,512,4,72]{1,3,2,0:T(8,128)(2,1)}, f32[4,2048,4,72]{1,3,2,0:T(8,128)}, f32[4,2048,4,72]{1,3,2,0:T(8,128)}, bf16[4,2048,4,72]{...) while((s32[]{:T(128)}, ...), condition=%wide.region_15.15_spmd, body=%wide.region_13.14_spmd.sunk | while | flops 3070965760 | bytes 169473184 | solution.py:113
  1032.3 13.2 constant_dynamic-update-slice_fusion.18
  1058.4 153.1 %while.57 = (s32[]{:T(128)}, bf16[4,512,4,72]{1,3,2,0:T(8,128)(2,1)}, f32[4,2048,4,72]{1,3,2,0:T(8,128)}, f32[4,2048,4,72]{1,3,2,0:T(8,128)}, bf16[4,2048,4,72]{...) while((s32[]{:T(128)}, ...), condition=%wide.region_15.15_spmd, body=%wide.region_13.14_spmd.sunk | while | flops 3070965760 | bytes 169473184 | solution.py:113
  1232.6 13.4 constant_dynamic-update-slice_fusion.18
  1254.3 25.8 fusion.52
  1280.9 18.6 fusion.51
  1299.5 84.6 %reduce-scatter.10.cloned.1.call-done = f32[2,512,1152]{2,1,0:T(8,128)} async-done(((f32[2,2048,1152]{2,1,0:T(8,128)}), f32[2,512,1152]{2,1,0:T(8,128)}) %reduce-scatter.10.cloned.1.call-update) | async-done | bytes 4718608 | tf_op jit(solution)/shard_map/reduce_scatter | solution.py:269
  1388.2 136.4 %reduce-scatter.8.cloned.1.call-done = f32[2,512,1152]{2,1,0:T(8,128)} async-done(((f32[2,2048,1152]{2,1,0:T(8,128)}), f32[2,512,1152]{2,1,0:T(8,128)}) %reduce-scatter.8.cloned.1.call-update) | async-done | bytes 4718608 | tf_op jit(solution)/shard_map/reduce_scatter | solution.py:268
  1541.7 16.0 fusion.87
  1584.5 107.0 %reduce-scatter.20.cloned.1.call-done = bf16[2304,1152]{1,0:T(8,128)(2,1)} async-done(((bf16[4608,1152]{1,0:T(8,128)(2,1)}), bf16[2304,1152]{1,0:T(8,128)(2,1)}) %reduce-scatter.20.cloned.1.call-update) | async-done | bytes 5308432 | tf_op jit(solution)/shard_map/reduce_scatter | solution.py:329
  1691.6 126.1 %reduce-scatter.18.cloned.1.call-done = bf16[576,4608]{1,0:T(8,128)(2,1)} async-done(((bf16[1152,4608]{1,0:T(8,128)(2,1)}), bf16[576,4608]{1,0:T(8,128)(2,1)}) %reduce-scatter.18.cloned.1.call-update) | async-done | bytes 5308432 | tf_op jit(solution)/shard_map/reduce_scatter | solution.py:323
  1817.7 97.7 %reduce-scatter.14.cloned.1.call-done = bf16[576,3456]{1,0:T(8,128)(2,1)} async-done(((bf16[1152,3456]{1,0:T(8,128)(2,1)}), bf16[576,3456]{1,0:T(8,128)(2,1)}) %reduce-scatter.14.cloned.1.call-update) | async-done | bytes 3981328 | tf_op jit(solution)/shard_map/reduce_scatter | solution.py:311
  1915.5 182.7 %reduce-scatter.12.cloned.1.call-done = bf16[576,6912]{1,0:T(8,128)(2,1)} async-done(((bf16[1152,6912]{1,0:T(8,128)(2,1)}), bf16[576,6912]{1,0:T(8,128)(2,1)}) %reduce-scatter.12.cloned.1.call-update) | async-done | bytes 7962640 | tf_op jit(solution)/shard_map/reduce_scatter | solution.py:305
  2112.0 63.2 %all-reduce.7 = (bf16[3456]{0:T(1024)(128)(2,1)S(1)}, bf16[1152]{0:T(1024)(128)(2,1)S(1)}, bf16[576]{0:T(1024)(128)(2,1)S(1)}, bf16[2304]{0:T(1024)(128)(2,1)S(1)}, bf16[576]{0:T(1024)(128)(2,1)S(1)}) all-reduce(bf16[3456]{0:T(1024)(128)(2,1)S(1)} %dynamic-slice.3, ...), channel_id=1, replica_groups=mesh['group'=2,'replica'=4,'seq'=4] {'replica','seq'}, use_global_device_ids=true, to_apply=%region_32.33 | all-reduce | flops 8064 | bytes 32256 | tf_op jit(solution)/shard_map/psum | solution.py:338
  2188.8 198.2 %all-reduce.13.cloned.1.call-done = (bf16[576,3456]{1,0:T(8,128)(2,1)}, bf16[576,1152]{1,0:T(8,128)(2,1)}, bf16[576,4608]{1,0:T(8,128)(2,1)}, bf16[2304,1152]{1,0:T(8,128)(2,1)}) async-done(((bf16[576,3456]{1,0:T(8,128)(2,1)}, bf16[576,1152]{1,0:T(8,128)(2,1)}, bf16[576,4608]{1,0:T(8,128)(2,1)}, bf16[2304,1152]{1,0:T(8,128)(2,1)}), (bf16[576,3456]{1,0:T(8,128)(2,1)}, bf16[576,1152]{1,0:T(8,128)(2,1)}, ...) | async-done | bytes 15925264 | tf_op jit(solution)/shard_map/psum | solution.py:339
  2408.1 590.5 %all-gather.27.cloned.1.call-done = bf16[9216,6912]{1,0:T(8,128)(2,1)} async-done(((bf16[576,6912]{1,0:T(8,128)(2,1)}), bf16[9216,6912]{1,0:T(8,128)(2,1)}) %all-gather.27.cloned.1.call-update) | async-done | bytes 127402000 | tf_op jit(solution)/shard_map/all_gather | solution.py:10
  2998.6 43.4 %reduce_sum.224 = bf16[576,6912]{1,0:T(8,128)(2,1)} reduce(bf16[16,576,6912]{2,1,0:T(8,128)(2,1)} %bitcast.48, bf16[]{:T(256)} %constant.123.clone.1), dimensions={0}, to_apply=%region_29.30 | reduce | flops 59719680 | bytes 135364608 | tf_op jit(solution)/shard_map/reduce_sum | solution.py:10
  (420 shorter events, 718.9 us)
Async XLA Ops:
  7.2 194.4 %all-gather.13.cloned.1.call-start = ((), (), s32[]{:S(2)}) async-start(), calls=%async_computation.7 | async-start | bytes 23887872 | tf_op jit(solution)/shard_map/all_gather | solution.py:154
  7.9 193.6 %copy-start.19 = (bf16[2,1152]{1,0:T(2,128)(2,1)S(1)}, bf16[2,1152]{1,0:T(2,128)(2,1)}, u32[]{:S(2)}) copy-start(bf16[2,1152]{1,0:T(2,128)(2,1)} %param.22) | copy-start | bytes 13828
  8.0 294.4 %all-gather.15.cloned.1.call-start = ((), (), s32[]{:S(2)}) async-start(), calls=%async_computation.8 | async-start | bytes 11943936 | tf_op jit(solution)/shard_map/all_gather | solution.py:156
  8.7 373.9 %all-gather.19.cloned.1.call-start = ((), (), s32[]{:S(2)}) async-start(), calls=%async_computation.10 | async-start | bytes 11796480 | tf_op jit(solution)/shard_map/all_gather | solution.py:201
  19.1 283.2 %copy-start.31 = (f32[2,512]{1,0:T(2,128)}, f32[2,512]{1,0:T(2,128)S(1)}, u32[]{:S(2)}) copy-start(f32[2,512]{1,0:T(2,128)S(1)} %broadcast_multiply_fusion.5) | copy-start | bytes 12292
  19.9 282.4 %copy-start.39 = (f32[2,512]{1,0:T(2,128)}, f32[2,512]{1,0:T(2,128)S(1)}, u32[]{:S(2)}) copy-start(f32[2,512]{1,0:T(2,128)S(1)} %add_rsqrt_fusion.1) | copy-start | bytes 12292
  209.9 105.1 %copy-start.42 = (f32[2,1152]{1,0:T(2,128)}, f32[2,1152]{1,0:T(2,128)S(1)}, u32[]{:S(2)}) copy-start(f32[2,1152]{1,0:T(2,128)S(1)} %get-tuple-element.311) | copy-start | bytes 27652
  318.2 130.6 %all-gather.17.cloned.1.call-start = ((), (), s32[]{:S(2)}) async-start(), calls=%async_computation.9 | async-start | bytes 11796480 | tf_op jit(solution)/shard_map/all_gather | solution.py:200
  318.8 275.1 %all-gather.21.cloned.1.call-start = ((), (), s32[]{:S(2)}) async-start(), calls=%async_computation.11 | async-start | bytes 3981312 | tf_op jit(solution)/shard_map/all_gather | solution.py:158
  319.4 302.6 %all-gather.23.cloned.1.call-start = ((), (), s32[]{:S(2)}) async-start(), calls=%async_computation.12 | async-start | bytes 15925248 | tf_op jit(solution)/shard_map/all_gather | solution.py:160
  320.0 434.5 %all-gather.25.cloned.1.call-start = ((), (), s32[]{:S(2)}) async-start(), calls=%async_computation.13 | async-start | bytes 15925248 | tf_op jit(solution)/shard_map/all_gather | solution.py:162
  320.7 1063.4 %reduce-scatter.10.cloned.1.call-start = ((), (), s32[]{:S(2)}) async-start(), calls=%async_computation.15 | async-start | bytes 23592960 | tf_op jit(solution)/shard_map/reduce_scatter | solution.py:269
  461.6 132.3 %copy-start.29 = (f32[2,1152]{1,0:T(2,128)S(1)}, f32[2,1152]{1,0:T(2,128)}, u32[]{:S(2)}) copy-start(f32[2,1152]{1,0:T(2,128)} %get-tuple-element.313) | copy-start | bytes 27652
  604.1 225.5 %copy-start.21 = (f32[2,512]{1,0:T(2,128)}, f32[2,512]{1,0:T(2,128)S(1)}, u32[]{:S(2)}) copy-start(f32[2,512]{1,0:T(2,128)S(1)} %broadcast_multiply_fusion.4) | copy-start | bytes 12292
  606.9 222.7 %copy-start.37 = (f32[2,512]{1,0:T(2,128)}, f32[2,512]{1,0:T(2,128)S(1)}, u32[]{:S(2)}) copy-start(f32[2,512]{1,0:T(2,128)S(1)} %add_rsqrt_fusion) | copy-start | bytes 12292
  622.0 132.5 %copy-start.15 = (bf16[2,512,1152]{2,1,0:T(8,128)(2,1)S(1)}, bf16[2,512,1152]{2,1,0:T(8,128)(2,1)}, u32[]{:S(2)}) copy-start(bf16[2,512,1152]{2,1,0:T(8,128)(2,1)} %param.33) | copy-start | bytes 7077892
  622.0 132.5 %copy-start.27 = (f32[2,1152]{1,0:T(2,128)S(1)}, f32[2,1152]{1,0:T(2,128)}, u32[]{:S(2)}) copy-start(f32[2,1152]{1,0:T(2,128)} %get-tuple-element.308) | copy-start | bytes 27652
  622.0 132.5 %copy-start.33 = (f32[4608]{0:T(1024)S(1)}, f32[4608]{0:T(1024)}, u32[]{:S(2)}) copy-start(f32[4608]{0:T(1024)} %reshape.181) | copy-start | bytes 55300
  1246.2 278.4 %reduce-scatter.8.cloned.1.call-start = ((), (), s32[]{:S(2)}) async-start(), calls=%async_computation.14 | async-start | bytes 23592960 | tf_op jit(solution)/shard_map/reduce_scatter | solution.py:268
  1246.9 337.6 %reduce-scatter.16.cloned.1.call-start = ((), (), s32[]{:S(2)}) async-start(), calls=%async_computation.18 | async-start | bytes 3981312 | tf_op jit(solution)/shard_map/reduce_scatter | solution.py:317
  1254.3 437.3 %reduce-scatter.20.cloned.1.call-start = ((), (), s32[]{:S(2)}) async-start(), calls=%async_computation.20 | async-start | bytes 15925248 | tf_op jit(solution)/shard_map/reduce_scatter | solution.py:329
  1280.2 537.5 %reduce-scatter.18.cloned.1.call-start = ((), (), s32[]{:S(2)}) async-start(), calls=%async_computation.19 | async-start | bytes 15925248 | tf_op jit(solution)/shard_map/reduce_scatter | solution.py:323
  1299.5 615.9 %reduce-scatter.14.cloned.1.call-start = ((), (), s32[]{:S(2)}) async-start(), calls=%async_computation.17 | async-start | bytes 11943936 | tf_op jit(solution)/shard_map/reduce_scatter | solution.py:311
  1384.1 144.6 %copy-start.24 = (f32[2,1152]{1,0:T(2,128)S(1)}, f32[2,1152]{1,0:T(2,128)}, u32[]{:S(2)}) copy-start(f32[2,1152]{1,0:T(2,128)} %copy-done.23) | copy-start | bytes 27652
  1384.1 144.6 %copy-start.32 = (f32[2,512]{1,0:T(2,128)S(1)}, f32[2,512]{1,0:T(2,128)}, u32[]{:S(2)}) copy-start(f32[2,512]{1,0:T(2,128)} %copy-done.31) | copy-start | bytes 12292
  1384.1 144.6 %copy-start.40 = (f32[2,512]{1,0:T(2,128)S(1)}, f32[2,512]{1,0:T(2,128)}, u32[]{:S(2)}) copy-start(f32[2,512]{1,0:T(2,128)} %copy-done.39) | copy-start | bytes 12292
  1384.1 144.6 %copy-start.43 = (f32[2,1152]{1,0:T(2,128)S(1)}, f32[2,1152]{1,0:T(2,128)}, u32[]{:S(2)}) copy-start(f32[2,1152]{1,0:T(2,128)} %copy-done.42) | copy-start | bytes 27652
  1388.2 140.6 %copy-start.9 = (bf16[2,512,1152]{2,1,0:T(8,128)(2,1)S(1)}, bf16[2,512,1152]{2,1,0:T(8,128)(2,1)}, u32[]{:S(2)}) copy-start(bf16[2,512,1152]{2,1,0:T(8,128)(2,1)} %param.21) | copy-start | bytes 7077892
  1541.5 556.7 %reduce-scatter.12.cloned.1.call-start = ((), (), s32[]{:S(2)}) async-start(), calls=%async_computation.16 | async-start | bytes 23887872 | tf_op jit(solution)/shard_map/reduce_scatter | solution.py:305
  1584.5 802.5 %all-reduce.13.cloned.1.call-start = ((), (), s32[]{:S(2)}) async-start(), calls=%async_computation.22 | async-start | bytes 31850496 | tf_op jit(solution)/shard_map/psum | solution.py:339
  1915.4 185.1 %copy-start.12 = (bf16[2,512,1152]{2,1,0:T(8,128)(2,1)S(1)}, bf16[2,512,1152]{2,1,0:T(8,128)(2,1)}, u32[]{:S(2)}) copy-start(bf16[2,512,1152]{2,1,0:T(8,128)(2,1)} %convert.21) | copy-start | bytes 7077892
  1915.4 1083.2 %all-gather.27.cloned.1.call-start = ((), (), s32[]{:S(2)}) async-start(), calls=%async_computation.21 | async-start | bytes 135364608 | tf_op jit(solution)/shard_map/all_gather | solution.py:10
  (71 other events, 637.6 us)
Sparse Core Ops, SparseCore 0:
  9.6 191.9 all-gather.12
  203.1 99.1 all-gather.14
  318.3 64.2 all-gather.18
  384.6 64.2 all-gather.16
  450.2 39.3 all-gather.20
  491.0 130.9 all-gather.22
  623.6 130.9 all-gather.24
  1246.3 137.8 reduce-scatter.9
  1386.7 137.8 reduce-scatter.7
  1527.3 38.0 reduce-scatter.15
  1568.2 123.3 reduce-scatter.19
  1694.3 123.3 reduce-scatter.17
  1820.6 94.7 reduce-scatter.13
  1918.1 180.0 reduce-scatter.11
  2102.6 284.3 all-reduce.12
  2388.4 610.1 all-gather.26
